TPU v7x, 32 devices: a whole 2x2x4 slice. The times are simulated.
32 devices in a mesh: seq: 16 (over z, y, core), dp: 2 (over x).
Axes of the slice: x: 2, y: 2, z: 4, core: 2. Of those that a mesh axis runs over, the one named last changes fastest.
Arguments:
- queries: bfloat16 [2, 2048, 1024], P('dp', 'seq'), may hold values from -6 to 6
- keys: bfloat16 [2, 2048, 1024], P('dp', 'seq'), may hold values from -6 to 6
- values: bfloat16 [2, 2048, 1024], P('dp', 'seq'), may hold values from -6 to 6
- d_out: bfloat16 [2, 2048, 1024], P('dp', 'seq'), may hold values from -6 to 6
- segment_ids: int32 [2, 2048], P('dp', 'seq'), may hold values from 0 to 2, never falling along the last dimension, each value on 1 to 1536 neighbouring positions
- block_bucket: int32 [2, 16], P('dp', 'seq'), may hold values from 0 to 63
- block_mask: int32 [2, 16, 5, 1], P('dp', 'seq'), may hold values 0 or 1
- bias_table: bfloat16 [16, 64, 64], replicated, may hold values from -4 to 4
Outputs:
- attention_out: bfloat16 [2, 2048, 1024], P('dp', 'seq')
- d_queries: bfloat16 [2, 2048, 1024], P('dp', 'seq')
- d_keys: bfloat16 [2, 2048, 1024], P('dp', 'seq')
- d_values: bfloat16 [2, 2048, 1024], P('dp', 'seq')
- d_table: float32 [16, 64, 64], replicated
Inputs may be any that keep to these rules, and one draw needn't show every extreme that they name: `segment_ids`: each document is a run of consecutive tokens of one sequence.
All inputs are finite; a program needn't handle non-finite values. No bound on the sum of `block_mask` on one device may be relied on, other than what follows from the above.
Results may differ from a plain program's by a relative error of at most 0.024.
Values may be sent and summed in bfloat16 or wider, within the bound.
No kernel may reach another device: no remote copies, remote signals or barrier semaphores. Data moves between devices by JAX's collectives and lax.ppermute only.
A program may use at most 64 MiB of HBM per device.

v0:
```python
import jax
import jax.numpy as jnp
from jax import lax
from jax.sharding import PartitionSpec as P

H = 16
DH = 64
NB = 64
BLK = 128
masked_value = -1e30


def from_partner(value, axis, apart):
    mask = 2**apart
    pairs = [(source, source ^ mask) for source in range(lax.axis_size(axis))]
    return lax.ppermute(value, axis, pairs)


def expand_blocks(bias_block, row_count, col_count):
    leading = bias_block.shape[:-2]
    row_blocks = bias_block.shape[-2]
    col_blocks = bias_block.shape[-1]
    widened = jnp.broadcast_to(
        bias_block[..., :, None, :, None],
        leading + (row_blocks, row_count // row_blocks, col_blocks, col_count // col_blocks),
    )
    return widened.reshape(leading + (row_count, col_count))


def one_hot_rows(buckets):
    levels_all = jnp.arange(NB, dtype=jnp.float32)
    return (buckets.astype(jnp.float32)[:, None] == levels_all[None, :]).astype(jnp.bfloat16)


def bias_tile(bias_table, row_hot, col_hot):
    picked = jnp.einsum(
        "bn,hnm->hbm", row_hot, bias_table, preferred_element_type=jnp.float32
    ).astype(jnp.bfloat16)
    return jnp.einsum("hbm,cm->hbc", picked, col_hot, preferred_element_type=jnp.float32)


def allowed_pairs(seg_rows, seg_cols, block_ok):
    same_doc = seg_rows.astype(jnp.float32)[:, None] == seg_cols.astype(jnp.float32)[None, :]
    return same_doc & expand_blocks(block_ok, seg_rows.shape[0], seg_cols.shape[0])


def masked_scores(query_heads, key_heads, bias_block, allowed):
    products = jnp.einsum(
        "thd,uhd->htu", query_heads, key_heads, preferred_element_type=jnp.float32
    )
    shifted = products * 0.125 + expand_blocks(bias_block, query_heads.shape[0], key_heads.shape[0])
    return jnp.where(allowed[None], shifted, masked_value)


def grad_terms(scores, allowed, lse, row_delta, grad_heads, value_heads):
    probs = jnp.where(allowed[None], jnp.exp(scores - lse[:, :, None]), 0.0)
    dprob = jnp.einsum("thd,uhd->htu", grad_heads, value_heads, preferred_element_type=jnp.float32)
    dscore = probs * (dprob - row_delta[:, :, None])
    return (probs.astype(jnp.bfloat16), dscore)


def local(queries, keys, values, d_out, segment_ids, block_bucket, block_mask, bias_table):
    row_count = queries.shape[1]
    block_count = row_count // BLK
    level_count = lax.axis_size("seq").bit_length() - 1
    query_heads = queries[0].reshape(row_count, H, DH)
    grad_heads = d_out[0].reshape(row_count, H, DH)
    own_keys = keys[0]
    own_values = values[0]
    own_seg = segment_ids[0]
    own_bucket = block_bucket[0]
    own_mask = block_mask[0] != 0
    own_hot = one_hot_rows(own_bucket)
    own_hot_wide = own_hot.astype(jnp.float32)
    section_list = list(range(level_count + 1))
    stored = {}
    run_max = jnp.full((H, row_count), masked_value, jnp.float32)
    run_sum = jnp.zeros((H, row_count), jnp.float32)
    run_acc = jnp.zeros((row_count, H, DH), jnp.float32)
    for section_num in section_list:
        if section_num == 0:
            key_rows, value_rows, seg_cols, bucket_cols = (
                own_keys,
                own_values,
                own_seg,
                own_bucket,
            )
            block_ok = own_mask[:, 0, :] | jnp.eye(block_count, dtype=bool)
        else:
            key_rows, value_rows, seg_cols, bucket_cols = from_partner(
                (
                    own_keys,
                    own_values,
                    own_seg.astype(jnp.bfloat16),
                    own_bucket.astype(jnp.bfloat16),
                ),
                "seq",
                section_num - 1,
            )
            block_ok = own_mask[:, section_num, :]
        key_heads = key_rows.reshape(row_count, H, DH)
        value_heads = value_rows.reshape(row_count, H, DH)
        col_hot = one_hot_rows(bucket_cols)
        bias_block = bias_tile(bias_table, own_hot, col_hot)
        allowed = allowed_pairs(own_seg, seg_cols, block_ok)
        stored[section_num] = (key_heads, value_heads, seg_cols, col_hot, bias_block, allowed)
        scores = masked_scores(query_heads, key_heads, bias_block, allowed)
        fresh_max = jnp.maximum(run_max, jnp.max(scores, axis=-1))
        rescale = jnp.exp(run_max - fresh_max)
        weights = jnp.where(allowed[None], jnp.exp(scores - fresh_max[:, :, None]), 0.0)
        run_sum = run_sum * rescale + jnp.sum(weights, axis=-1)
        run_acc = run_acc * rescale.T[:, :, None] + jnp.einsum(
            "htu,uhd->thd",
            weights.astype(jnp.bfloat16),
            value_heads,
            preferred_element_type=jnp.float32,
        )
        run_max = fresh_max
    out_heads = (run_acc / run_sum.T[:, :, None]).astype(jnp.bfloat16)
    lse = run_max + jnp.log(run_sum)
    row_delta = jnp.sum(out_heads.astype(jnp.float32) * grad_heads.astype(jnp.float32), axis=-1).T
    out_rows = out_heads.reshape(row_count, H * DH)
    query_acc = jnp.zeros((row_count, H, DH), jnp.float32)
    key_acc = jnp.zeros((row_count, H, DH), jnp.float32)
    value_acc = jnp.zeros((row_count, H, DH), jnp.float32)
    table_acc = jnp.zeros((H, NB, NB), jnp.float32)
    for section_num in section_list:
        key_heads, value_heads, seg_cols, col_hot, bias_block, allowed = stored[section_num]
        scores = masked_scores(query_heads, key_heads, bias_block, allowed)
        probs_low, dscore = grad_terms(scores, allowed, lse, row_delta, grad_heads, value_heads)
        dscore_low = dscore.astype(jnp.bfloat16)
        query_acc = (
            query_acc
            + jnp.einsum("htu,uhd->thd", dscore_low, key_heads, preferred_element_type=jnp.float32)
            * 0.125
        )
        block_sums = dscore.reshape(H, block_count, BLK, block_count, BLK).sum(axis=(2, 4))
        table_acc = table_acc + jnp.einsum(
            "bn,hbc,cm->hnm",
            own_hot_wide,
            block_sums,
            col_hot.astype(jnp.float32),
            precision=lax.Precision.HIGHEST,
        )
        if section_num == 0:
            key_acc = (
                jnp.einsum(
                    "htu,thd->uhd", dscore_low, query_heads, preferred_element_type=jnp.float32
                )
                * 0.125
            )
            value_acc = jnp.einsum(
                "htu,thd->uhd", probs_low, grad_heads, preferred_element_type=jnp.float32
            )
        else:
            key_term = (
                jnp.einsum(
                    "htu,thd->uhd", dscore_low, query_heads, preferred_element_type=jnp.float32
                )
                * 0.125
            ).astype(jnp.bfloat16)
            value_term = jnp.einsum(
                "htu,thd->uhd", probs_low, grad_heads, preferred_element_type=jnp.float32
            ).astype(jnp.bfloat16)
            back_keys, back_values = from_partner(
                (key_term.reshape(row_count, H * DH), value_term.reshape(row_count, H * DH)),
                "seq",
                section_num - 1,
            )
            key_acc = key_acc + back_keys.reshape(row_count, H, DH).astype(jnp.float32)
            value_acc = value_acc + back_values.reshape(row_count, H, DH).astype(jnp.float32)
    table_total = lax.psum(table_acc, ("seq", "dp"))
    feature_count = H * DH
    return (
        out_rows.reshape(1, row_count, feature_count),
        query_acc.astype(jnp.bfloat16).reshape(1, row_count, feature_count),
        key_acc.astype(jnp.bfloat16).reshape(1, row_count, feature_count),
        value_acc.astype(jnp.bfloat16).reshape(1, row_count, feature_count),
        table_total,
    )


def solution(mesh):
    in_specs = (
        P("dp", "seq", None),
        P("dp", "seq", None),
        P("dp", "seq", None),
        P("dp", "seq", None),
        P("dp", "seq"),
        P("dp", "seq"),
        P("dp", "seq", None, None),
        P(),
    )
    out_specs = (
        P("dp", "seq", None),
        P("dp", "seq", None),
        P("dp", "seq", None),
        P("dp", "seq", None),
        P(),
    )
    return jax.shard_map(local, mesh=mesh, in_specs=in_specs, out_specs=out_specs, check_vma=False)
```

profile of v0, /device:TPU:0, one launch (start us, length us, event | category | flops | bytes accessed | tf_op | source)
XLA Modules:
  0.0 256.8 jit_solution(7733567742736410515)
XLA Ops:
  7.2 0.7 convert_bitcast_fusion
  8.0 3.0 %collective-permute-start.4 = (bf16[128]{0:T(256)(128)(2,1)S(1)}, bf16[128]{0:T(256)(128)(2,1)S(1)}, u32[]{:S(2)}, u32[]{:S(2)}) collective-permute-start(bf16[128]{0:T(256)(128)(2,1)S(1)} %get-tuple-element.40), channel_id=1, source_target_pairs={{0,4},{2,6},{4,0},{6,2},{8,12},{10,14},{12,8},{14,10},{16,20},{18,... | collective-permute-start | bytes 776 | tf_op jit(solution)/shard_map/ppermute | solution.py:16
  10.9 1.6 collective-permute-start.8
  12.5 2.6 %collective-permute-start.12 = (bf16[128]{0:T(256)(128)(2,1)S(1)}, bf16[128]{0:T(256)(128)(2,1)S(1)}, u32[]{:S(2)}, u32[]{:S(2)}) collective-permute-start(bf16[128]{0:T(256)(128)(2,1)S(1)} %get-tuple-element.40), channel_id=1, source_target_pairs={{0,16},{2,18},{4,20},{6,22},{8,24},{10,26},{12,28},{14,30},{16,0},... | collective-permute-start | bytes 776 | tf_op jit(solution)/shard_map/ppermute | solution.py:16
  15.8 1.7 collective-permute-start.14
  17.5 1.1 copy.81
  20.9 1.1 copy.66
  22.0 1.1 copy.67
  23.2 1.8 collective-permute-start.10
  25.8 1.0 collective-permute-done.10
  26.7 1.8 collective-permute-start.6
  30.2 0.8 collective-permute-start.2
  31.8 2.6 %collective-permute-start.13 = (bf16[128,1024]{1,0:T(8,128)(2,1)}, bf16[128,1024]{1,0:T(8,128)(2,1)S(1)}, u32[]{:S(2)}, u32[]{:S(2)}) collective-permute-start(bf16[128,1024]{1,0:T(8,128)(2,1)} %bitcast.15), channel_id=1, source_target_pairs={{0,16},{2,18},{4,20},{6,22},{8,24},{10,26},{12,28},{14,30},{16,0},... | collective-permute-start | bytes 786440 | tf_op jit(solution)/shard_map/ppermute | solution.py:16
  36.4 1.2 collective-permute-start.5
  38.0 2.6 %broadcast_compare_fusion = (pred[128,128]{0,1:T(8,128)(4,1)S(1)}, pred[128,128]{0,1:T(8,128)(4,1)S(1)}, pred[128,128]{0,1:T(8,128)(4,1)S(1)}, pred[128,128]{0,1:T(8,128)(4,1)S(1)}, pred[128,128]{0,1:T(8,128)(4,1)S(1)}) fusion(f32[128]{0:T(128)S(1)} %get-tuple-element.41, pred[]{:T(512)} %bitcast.25, f32[128]{0:T(128)S(1)} %convert_element_type.245, ...), kind=kLoop, calls=%fused_computation.151 | loop fusion | flops 147456 | bytes 84484 | tf_op jit(solution)/shard_map/eq | solution.py:43
  41.1 6.8 %collective-permute-done.13 = bf16[128,1024]{1,0:T(8,128)(2,1)S(1)} collective-permute-done((bf16[128,1024]{1,0:T(8,128)(2,1)}, bf16[128,1024]{1,0:T(8,128)(2,1)S(1)}, u32[]{:S(2)}, u32[]{:S(2)}) %collective-permute-start.13) | collective-permute-done | bytes 262176 | tf_op jit(solution)/shard_map/ppermute | solution.py:16
  47.8 0.8 copy.78
  48.7 1.3 fusion.150
  50.2 1.2 collective-permute-start.7
  51.4 1.8 copy.75
  53.2 2.3 fusion.151
  55.5 1.8 copy.72
  57.3 2.3 fusion.152
  59.6 1.8 copy.69
  61.4 1.5 fusion.153
  64.9 1.1 fusion.16
  66.0 1.8 copy.79
  67.8 2.0 convolution_bitcast_fusion
  69.9 1.8 copy.76
  71.7 2.4 convolution_bitcast_fusion.1
  74.1 1.8 copy.73
  75.8 2.4 convolution_bitcast_fusion.2
  78.3 1.8 copy.70
  80.1 0.7 copy-done.24
  80.8 3.1 %multiply_reduce_fusion = (f32[128,16]{0,1:T(8,128)S(1)}, bf16[128,16,64]{0,2,1:T(8,128)(2,1)}) fusion(bf16[128,16,64]{0,2,1:T(8,128)(2,1)S(1)} %bitcast.299, f32[128,16]{0,1:T(8,128)S(1)} %copy-done.24, f32[128,16,64]{0,2,1:T(8,128)} %convolution_bitcast_fusion, f32[128,16]{0,1:T(8,128)S(1)} %copy-done.27, f32[128,16,64]{0,2,1:T(8,128)} %convolution_bitcast_fusion.1, ...), kind=kOutput, calls=%fused_computation.103 | convolution fusion | flops 36042752 | bytes 3997696 | tf_op jit(solution)/shard_map/htu,uhd->thd/dot_general | solution.py:112
  87.0 1.3 fusion.156
  88.3 1.3 fusion.157
  89.6 1.1 fusion.93
  90.7 1.2 fusion.32
  91.9 1.1 fusion.96
  92.9 1.2 fusion.31
  94.1 1.1 fusion.103
  95.6 1.2 convolution_convert_fusion
  96.8 1.2 convolution_convert_fusion.1
  98.0 1.2 convolution_convert_fusion.2
  99.8 1.9 copy.102
  101.6 1.2 fusion.29
  103.1 0.8 copy-done.8
  103.9 1.2 fusion.30
  105.1 1.0 fusion.33
  106.1 1.9 copy.103
  108.0 2.9 %collective-permute-start.19 = (bf16[128,1024]{0,1:T(8,128)(2,1)}, bf16[128,1024]{0,1:T(8,128)(2,1)}, u32[]{:S(2)}, u32[]{:S(2)}) collective-permute-start(bf16[128,1024]{0,1:T(8,128)(2,1)} %bitcast.353), channel_id=1, source_target_pairs={{0,16},{2,18},{4,20},{6,22},{8,24},{10,26},{12,28},{14,30},{16,0},... | collective-permute-start | bytes 786440 | tf_op jit(solution)/shard_map/ppermute | solution.py:16
  110.9 0.8 collective-permute-start.17
  111.7 2.0 collective-permute-start.23
  113.8 1.5 multiply_add_fusion
  115.9 8.2 %collective-permute-done.19 = bf16[128,1024]{0,1:T(8,128)(2,1)} collective-permute-done((bf16[128,1024]{0,1:T(8,128)(2,1)}, bf16[128,1024]{0,1:T(8,128)(2,1)}, u32[]{:S(2)}, u32[]{:S(2)}) %collective-permute-start.19) | collective-permute-done | bytes 262176 | tf_op jit(solution)/shard_map/ppermute | solution.py:16
  124.6 1.2 collective-permute-start.21
  125.8 1.4 fusion.61
  127.2 9.0 %collective-permute-done.23 = bf16[128,1024]{0,1:T(8,128)(2,1)S(1)} collective-permute-done((bf16[128,1024]{0,1:T(8,128)(2,1)}, bf16[128,1024]{0,1:T(8,128)(2,1)S(1)}, u32[]{:S(2)}, u32[]{:S(2)}) %collective-permute-start.23) | collective-permute-done | bytes 262176 | tf_op jit(solution)/shard_map/ppermute | solution.py:16
  136.2 1.1 collective-permute-done.22
  137.5 0.8 copy.104
  138.4 0.8 copy.105
  139.2 108.9 %all-reduce.2.cloned.1.call-done = f32[16,64,64]{2,1,0:T(8,128)} async-done(((f32[16,64,64]{2,1,0:T(8,128)}), f32[16,64,64]{2,1,0:T(8,128)}) %all-reduce.2.cloned.1.call-update) | async-done | bytes 262160 | tf_op jit(solution)/shard_map/psum | solution.py:172
  248.1 1.9 copy.134
  (130 shorter events, 13.8 us)
Async XLA Ops:
  7.2 12.0 %copy-start = (bf16[16,64,64]{2,1,0:T(8,128)(2,1)S(1)}, bf16[16,64,64]{2,1,0:T(8,128)(2,1)}, u32[]{:S(2)}) copy-start(bf16[16,64,64]{2,1,0:T(8,128)(2,1)} %param.15) | copy-start | bytes 393220
  7.2 240.9 %all-reduce.2.cloned.1.call-start = ((), (), s32[]{:S(2)}) async-start(), calls=%async_computation | async-start | bytes 1048576 | tf_op jit(solution)/shard_map/psum | solution.py:172
  8.0 27.9 %collective-permute-start.4 = (bf16[128]{0:T(256)(128)(2,1)S(1)}, bf16[128]{0:T(256)(128)(2,1)S(1)}, u32[]{:S(2)}, u32[]{:S(2)}) collective-permute-start(bf16[128]{0:T(256)(128)(2,1)S(1)} %get-tuple-element.40), channel_id=1, source_target_pairs={{0,4},{2,6},{4,0},{6,2},{8,12},{10,14},{12,8},{14,10},{16,20},{18,... | collective-permute-start | bytes 776 | tf_op jit(solution)/shard_map/ppermute | solution.py:16
  10.9 25.5 %collective-permute-start.8 = (bf16[128]{0:T(256)(128)(2,1)S(1)}, bf16[128]{0:T(256)(128)(2,1)S(1)}, u32[]{:S(2)}, u32[]{:S(2)}) collective-permute-start(bf16[128]{0:T(256)(128)(2,1)S(1)} %get-tuple-element.40), channel_id=1, source_target_pairs={{0,8},{2,10},{4,12},{6,14},{8,0},{10,2},{12,4},{14,6},{16,24},{18,... | collective-permute-start | bytes 776 | tf_op jit(solution)/shard_map/ppermute | solution.py:16
  12.5 25.1 %collective-permute-start.12 = (bf16[128]{0:T(256)(128)(2,1)S(1)}, bf16[128]{0:T(256)(128)(2,1)S(1)}, u32[]{:S(2)}, u32[]{:S(2)}) collective-permute-start(bf16[128]{0:T(256)(128)(2,1)S(1)} %get-tuple-element.40), channel_id=1, source_target_pairs={{0,16},{2,18},{4,20},{6,22},{8,24},{10,26},{12,28},{14,30},{16,0},... | collective-permute-start | bytes 776 | tf_op jit(solution)/shard_map/ppermute | solution.py:16
  15.1 22.5 %collective-permute-start = (bf16[128]{0:T(256)(128)(2,1)S(1)}, bf16[128]{0:T(256)(128)(2,1)S(1)}, u32[]{:S(2)}, u32[]{:S(2)}) collective-permute-start(bf16[128]{0:T(256)(128)(2,1)S(1)} %get-tuple-element.40), channel_id=1, source_target_pairs={{0,2},{2,0},{4,6},{6,4},{8,10},{10,8},{12,14},{14,12},{16,18},{18,... | collective-permute-start | bytes 776 | tf_op jit(solution)/shard_map/ppermute | solution.py:16
  15.8 7.4 %collective-permute-start.14 = (bf16[1]{0:T(256)(128)(2,1)}, bf16[1]{0:T(256)(128)(2,1)}, u32[]{:S(2)}, u32[]{:S(2)}) collective-permute-start(bf16[1]{0:T(256)(128)(2,1)} %bitcast.17), channel_id=1, source_target_pairs={{0,16},{2,18},{4,20},{6,22},{8,24},{10,26},{12,28},{14,30},{16,0},... | collective-permute-start | bytes 14 | tf_op jit(solution)/shard_map/ppermute | solution.py:16
  18.6 1.0 copy-start.22
  19.5 0.7 copy-start.33
  23.2 3.6 %collective-permute-start.10 = (bf16[1]{0:T(256)(128)(2,1)}, bf16[1]{0:T(256)(128)(2,1)}, u32[]{:S(2)}, u32[]{:S(2)}) collective-permute-start(bf16[1]{0:T(256)(128)(2,1)} %bitcast.17), channel_id=1, source_target_pairs={{0,8},{2,10},{4,12},{6,14},{8,0},{10,2},{12,4},{14,6},{16,24},{18,... | collective-permute-start | bytes 14 | tf_op jit(solution)/shard_map/ppermute | solution.py:16
  26.7 3.5 %collective-permute-start.6 = (bf16[1]{0:T(256)(128)(2,1)}, bf16[1]{0:T(256)(128)(2,1)}, u32[]{:S(2)}, u32[]{:S(2)}) collective-permute-start(bf16[1]{0:T(256)(128)(2,1)} %bitcast.17), channel_id=1, source_target_pairs={{0,4},{2,6},{4,0},{6,2},{8,12},{10,14},{12,8},{14,10},{16,20},{18,... | collective-permute-start | bytes 14 | tf_op jit(solution)/shard_map/ppermute | solution.py:16
  30.2 1.6 collective-permute-start.2
  31.8 16.0 %collective-permute-start.13 = (bf16[128,1024]{1,0:T(8,128)(2,1)}, bf16[128,1024]{1,0:T(8,128)(2,1)S(1)}, u32[]{:S(2)}, u32[]{:S(2)}) collective-permute-start(bf16[128,1024]{1,0:T(8,128)(2,1)} %bitcast.15), channel_id=1, source_target_pairs={{0,16},{2,18},{4,20},{6,22},{8,24},{10,26},{12,28},{14,30},{16,0},... | collective-permute-start | bytes 786440 | tf_op jit(solution)/shard_map/ppermute | solution.py:16
  35.8 14.4 %collective-permute-start.9 = (bf16[128,1024]{1,0:T(8,128)(2,1)}, bf16[128,1024]{1,0:T(8,128)(2,1)}, u32[]{:S(2)}, u32[]{:S(2)}) collective-permute-start(bf16[128,1024]{1,0:T(8,128)(2,1)} %bitcast.15), channel_id=1, source_target_pairs={{0,8},{2,10},{4,12},{6,14},{8,0},{10,2},{12,4},{14,6},{16,24},{18,... | collective-permute-start | bytes 786440 | tf_op jit(solution)/shard_map/ppermute | solution.py:16
  36.4 19.1 %collective-permute-start.5 = (bf16[128,1024]{1,0:T(8,128)(2,1)}, bf16[128,1024]{1,0:T(8,128)(2,1)}, u32[]{:S(2)}, u32[]{:S(2)}) collective-permute-start(bf16[128,1024]{1,0:T(8,128)(2,1)} %bitcast.15), channel_id=1, source_target_pairs={{0,4},{2,6},{4,0},{6,2},{8,12},{10,14},{12,8},{14,10},{16,20},{18,... | collective-permute-start | bytes 786440 | tf_op jit(solution)/shard_map/ppermute | solution.py:16
  37.6 22.0 %collective-permute-start.1 = (bf16[128,1024]{1,0:T(8,128)(2,1)}, bf16[128,1024]{1,0:T(8,128)(2,1)}, u32[]{:S(2)}, u32[]{:S(2)}) collective-permute-start(bf16[128,1024]{1,0:T(8,128)(2,1)} %bitcast.15), channel_id=1, source_target_pairs={{0,2},{2,0},{4,6},{6,4},{8,10},{10,8},{12,14},{14,12},{16,18},{18,... | collective-permute-start | bytes 786440 | tf_op jit(solution)/shard_map/ppermute | solution.py:16
  37.6 28.4 %collective-permute-start.15 = (bf16[128,1024]{1,0:T(8,128)(2,1)}, bf16[128,1024]{1,0:T(8,128)(2,1)}, u32[]{:S(2)}, u32[]{:S(2)}) collective-permute-start(bf16[128,1024]{1,0:T(8,128)(2,1)} %bitcast.22), channel_id=1, source_target_pairs={{0,16},{2,18},{4,20},{6,22},{8,24},{10,26},{12,28},{14,30},{16,0},... | collective-permute-start | bytes 786440 | tf_op jit(solution)/shard_map/ppermute | solution.py:16
  47.8 22.0 %collective-permute-start.11 = (bf16[128,1024]{1,0:T(8,128)(2,1)}, bf16[128,1024]{1,0:T(8,128)(2,1)}, u32[]{:S(2)}, u32[]{:S(2)}) collective-permute-start(bf16[128,1024]{1,0:T(8,128)(2,1)} %bitcast.22), channel_id=1, source_target_pairs={{0,8},{2,10},{4,12},{6,14},{8,0},{10,2},{12,4},{14,6},{16,24},{18,... | collective-permute-start | bytes 786440 | tf_op jit(solution)/shard_map/ppermute | solution.py:16
  50.2 23.9 %collective-permute-start.7 = (bf16[128,1024]{1,0:T(8,128)(2,1)}, bf16[128,1024]{1,0:T(8,128)(2,1)}, u32[]{:S(2)}, u32[]{:S(2)}) collective-permute-start(bf16[128,1024]{1,0:T(8,128)(2,1)} %bitcast.22), channel_id=1, source_target_pairs={{0,4},{2,6},{4,0},{6,2},{8,12},{10,14},{12,8},{14,10},{16,20},{18,... | collective-permute-start | bytes 786440 | tf_op jit(solution)/shard_map/ppermute | solution.py:16
  55.5 22.8 %collective-permute-start.3 = (bf16[128,1024]{1,0:T(8,128)(2,1)}, bf16[128,1024]{1,0:T(8,128)(2,1)}, u32[]{:S(2)}, u32[]{:S(2)}) collective-permute-start(bf16[128,1024]{1,0:T(8,128)(2,1)} %bitcast.22), channel_id=1, source_target_pairs={{0,2},{2,0},{4,6},{6,4},{8,10},{10,8},{12,14},{14,12},{16,18},{18,... | collective-permute-start | bytes 786440 | tf_op jit(solution)/shard_map/ppermute | solution.py:16
  61.4 1.7 copy-start.1
  61.4 1.7 copy-start.3
  62.9 1.0 copy-start.5
  78.3 1.8 copy-start.25
  78.3 1.8 copy-start.26
  78.3 1.8 copy-start.27
  80.1 0.7 copy-start.24
  80.8 3.1 %copy-start.18 = (bf16[128,1024]{0,1:T(8,128)(2,1)S(1)}, bf16[128,1024]{0,1:T(8,128)(2,1)}, u32[]{:S(2)}) copy-start(bf16[128,1024]{0,1:T(8,128)(2,1)} %copy.79) | copy-start | bytes 786436
  83.9 1.2 copy-start.2
  83.9 1.3 copy-start.19
  85.7 1.2 copy-start.6
  85.7 1.3 copy-start.23
  87.0 1.3 copy-start.4
  87.0 1.3 copy-start.17
  88.3 1.3 copy-start.14
  90.7 1.2 copy-start.16
  99.8 1.9 copy-start.9
  101.6 1.2 copy-start.12
  101.6 1.2 copy-start.15
  102.8 1.0 copy-start.8
  102.8 2.2 copy-start.13
  103.9 1.2 copy-start.10
  103.9 1.2 copy-start.11
  105.1 8.6 %copy-start.28 = (f32[64]{0:T(128)S(1)}, f32[64]{0:T(128)}, u32[]{:S(2)}) copy-start(f32[64]{0:T(128)} %fusion.128) | copy-start | bytes 772
  105.1 8.7 %copy-start.29 = (f32[64]{0:T(128)S(1)}, f32[64]{0:T(128)}, u32[]{:S(2)}) copy-start(f32[64]{0:T(128)} %get-tuple-element.68) | copy-start | bytes 772
  105.1 8.7 %copy-start.30 = (f32[64]{0:T(128)S(1)}, f32[64]{0:T(128)}, u32[]{:S(2)}) copy-start(f32[64]{0:T(128)} %get-tuple-element.69) | copy-start | bytes 772
  105.1 8.7 %copy-start.31 = (f32[64]{0:T(128)S(1)}, f32[64]{0:T(128)}, u32[]{:S(2)}) copy-start(f32[64]{0:T(128)} %get-tuple-element.70) | copy-start | bytes 772
  105.1 8.7 %copy-start.32 = (f32[64]{0:T(128)S(1)}, f32[64]{0:T(128)}, u32[]{:S(2)}) copy-start(f32[64]{0:T(128)} %get-tuple-element.71) | copy-start | bytes 772
  106.1 9.3 %copy-start.7 = (f32[16,128,128]{1,2,0:T(8,128)S(1)}, f32[16,128,128]{1,2,0:T(8,128)}, u32[]{:S(2)}) copy-start(f32[16,128,128]{1,2,0:T(8,128)} %copy-done.5) | copy-start | bytes 3145732
  108.0 16.1 %collective-permute-start.19 = (bf16[128,1024]{0,1:T(8,128)(2,1)}, bf16[128,1024]{0,1:T(8,128)(2,1)}, u32[]{:S(2)}, u32[]{:S(2)}) collective-permute-start(bf16[128,1024]{0,1:T(8,128)(2,1)} %bitcast.353), channel_id=1, source_target_pairs={{0,16},{2,18},{4,20},{6,22},{8,24},{10,26},{12,28},{14,30},{16,0},... | collective-permute-start | bytes 786440 | tf_op jit(solution)/shard_map/ppermute | solution.py:16
  110.9 13.7 %collective-permute-start.18 = (bf16[128,1024]{0,1:T(8,128)(2,1)}, bf16[128,1024]{0,1:T(8,128)(2,1)}, u32[]{:S(2)}, u32[]{:S(2)}) collective-permute-start(bf16[128,1024]{0,1:T(8,128)(2,1)} %bitcast.352), channel_id=1, source_target_pairs={{0,8},{2,10},{4,12},{6,14},{8,0},{10,2},{12,4},{14,6},{16,24},{18,... | collective-permute-start | bytes 786440 | tf_op jit(solution)/shard_map/ppermute | solution.py:16
  110.9 15.0 %collective-permute-start.17 = (bf16[128,1024]{0,1:T(8,128)(2,1)}, bf16[128,1024]{0,1:T(8,128)(2,1)}, u32[]{:S(2)}, u32[]{:S(2)}) collective-permute-start(bf16[128,1024]{0,1:T(8,128)(2,1)} %bitcast.355), channel_id=1, source_target_pairs={{0,4},{2,6},{4,0},{6,2},{8,12},{10,14},{12,8},{14,10},{16,20},{18,... | collective-permute-start | bytes 786440 | tf_op jit(solution)/shard_map/ppermute | solution.py:16
  111.7 14.1 %collective-permute-start.16 = (bf16[128,1024]{0,1:T(8,128)(2,1)}, bf16[128,1024]{0,1:T(8,128)(2,1)}, u32[]{:S(2)}, u32[]{:S(2)}) collective-permute-start(bf16[128,1024]{0,1:T(8,128)(2,1)} %bitcast.354), channel_id=1, source_target_pairs={{0,2},{2,0},{4,6},{6,4},{8,10},{10,8},{12,14},{14,12},{16,18},{18,... | collective-permute-start | bytes 786440 | tf_op jit(solution)/shard_map/ppermute | solution.py:16
  111.7 24.5 %collective-permute-start.23 = (bf16[128,1024]{0,1:T(8,128)(2,1)}, bf16[128,1024]{0,1:T(8,128)(2,1)S(1)}, u32[]{:S(2)}, u32[]{:S(2)}) collective-permute-start(bf16[128,1024]{0,1:T(8,128)(2,1)} %bitcast.343), channel_id=1, source_target_pairs={{0,16},{2,18},{4,20},{6,22},{8,24},{10,26},{12,28},{14,30},{16,0},... | collective-permute-start | bytes 786440 | tf_op jit(solution)/shard_map/ppermute | solution.py:16
  115.4 8.7 %copy-start.21 = (bf16[16,128,64]{1,2,0:T(8,128)(2,1)S(1)}, bf16[16,128,64]{1,2,0:T(8,128)(2,1)}, u32[]{:S(2)}) copy-start(bf16[16,128,64]{1,2,0:T(8,128)(2,1)} %convolution_convert_fusion.1) | copy-start | bytes 786436
  115.4 9.2 %copy-start.20 = (bf16[16,128,64]{1,2,0:T(8,128)(2,1)S(1)}, bf16[16,128,64]{1,2,0:T(8,128)(2,1)}, u32[]{:S(2)}) copy-start(bf16[16,128,64]{1,2,0:T(8,128)(2,1)} %convolution_convert_fusion.2) | copy-start | bytes 786436
  124.1 13.2 %collective-permute-start.22 = (bf16[128,1024]{0,1:T(8,128)(2,1)S(1)}, bf16[128,1024]{0,1:T(8,128)(2,1)S(1)}, u32[]{:S(2)}, u32[]{:S(2)}) collective-permute-start(bf16[128,1024]{0,1:T(8,128)(2,1)S(1)} %bitcast.342), channel_id=1, source_target_pairs={{0,8},{2,10},{4,12},{6,14},{8,0},{10,2},{12,4},{14,6},{16,24},{18,... | collective-permute-start | bytes 786440 | tf_op jit(solution)/shard_map/ppermute | solution.py:16
  124.6 12.7 %collective-permute-start.21 = (bf16[128,1024]{0,1:T(8,128)(2,1)S(1)}, bf16[128,1024]{0,1:T(8,128)(2,1)S(1)}, u32[]{:S(2)}, u32[]{:S(2)}) collective-permute-start(bf16[128,1024]{0,1:T(8,128)(2,1)S(1)} %bitcast.341), channel_id=1, source_target_pairs={{0,4},{2,6},{4,0},{6,2},{8,12},{10,14},{12,8},{14,10},{16,20},{18,... | collective-permute-start | bytes 786440 | tf_op jit(solution)/shard_map/ppermute | solution.py:16
  125.8 11.5 %collective-permute-start.20 = (bf16[128,1024]{0,1:T(8,128)(2,1)S(1)}, bf16[128,1024]{0,1:T(8,128)(2,1)S(1)}, u32[]{:S(2)}, u32[]{:S(2)}) collective-permute-start(bf16[128,1024]{0,1:T(8,128)(2,1)S(1)} %bitcast.345), channel_id=1, source_target_pairs={{0,2},{2,0},{4,6},{6,4},{8,10},{10,8},{12,14},{14,12},{16,18},{18,... | collective-permute-start | bytes 786440 | tf_op jit(solution)/shard_map/ppermute | solution.py:16
Sparse Core Ops, SparseCore 0:
  115.5 132.5 all-reduce.1
where the time goes:
time: 258 us; the launch traced here: 257 us
  waiting for transfers between devices  136 us (53%)
  matrix products  38.1 us (15%)
  local copies, waits for them, and re-layouts  28.9 us (11%)
  starting transfers between devices  26.2 us (10%)
  between operations  17.7 us (7%)
  other arithmetic  9.98 us (4%)
    psum x1, waiting for transfers between devices, local(): table_total = lax.psum(table_acc, ('seq', 'dp'))  109 us
    ppermute x24, waiting for transfers between devices, from_partner(): return lax.ppermute(value, axis, pairs)  27.1 us
    ppermute x24, starting transfers between devices, from_partner(): return lax.ppermute(value, axis, pairs)  26.2 us
    unnamed x77, local copies, waits for them, and re-layouts  14.8 us
    ppermute x8, local copies, waits for them, and re-layouts, from_partner(): return lax.ppermute(value, axis, pairs)  13.4 us
    dot_general x5, matrix products, local(): jnp.einsum('htu,uhd->thd', weights.astype(jnp.bfloat16), value_heads, pre...  11 us
    dot_general x5, matrix products, masked_scores(): jnp.einsum('thd,uhd->htu', query_heads, key_heads, preferred_element_type...  7.82 us
  transfers between devices with their start and end apart: 25, of which 9 were waited for; matrix products, arithmetic and copies ran while one was open for 17% of the time, Pallas kernels for 0%

commit v1 on v0

--- a/solution.py
+++ b/solution.py
@@ -169,7 +169,7 @@
             )
             key_acc = key_acc + back_keys.reshape(row_count, H, DH).astype(jnp.float32)
             value_acc = value_acc + back_values.reshape(row_count, H, DH).astype(jnp.float32)
-    table_total = lax.psum(table_acc, ("seq", "dp"))
+    table_total = lax.psum(lax.psum(table_acc, "dp"), "seq")
     feature_count = H * DH
     return (
         out_rows.reshape(1, row_count, feature_count),

time: 258 us -> 247 us (0.957)
  waiting for transfers between devices: 136 us -> 122 us
    ppermute x24, waiting for transfers between devices: 27.1 us -> 13.2 us  [from_partner(): return lax.ppermute(value, axis, pairs)]
    psum x1 -> x2, waiting for transfers between devices: 109 us -> 109 us  [local(): table_total = lax.psum(lax.psum(table_acc, 'dp'), 'seq')]
  transfers between devices with their start and end apart: 25 -> 26, of which waited for: 9 -> 8; matrix products, arithmetic and copies ran while one was open for 17% -> 18% of each run, Pallas kernels for 0% -> 0%
where the time goes in v1:
time: 247 us; the launch traced here: 246 us
  waiting for transfers between devices  122 us (49%)
  matrix products  38.8 us (16%)
  local copies, waits for them, and re-layouts  29.8 us (12%)
  starting transfers between devices  28 us (11%)
  between operations  17.7 us (7%)
  other arithmetic  9.97 us (4%)
    psum x2, waiting for transfers between devices, local(): table_total = lax.psum(lax.psum(table_acc, 'dp'), 'seq')  109 us
    ppermute x24, starting transfers between devices, from_partner(): return lax.ppermute(value, axis, pairs)  27.9 us
    unnamed x77, local copies, waits for them, and re-layouts  15.7 us
    ppermute x8, local copies, waits for them, and re-layouts, from_partner(): return lax.ppermute(value, axis, pairs)  13.4 us
    ppermute x24, waiting for transfers between devices, from_partner(): return lax.ppermute(value, axis, pairs)  13.2 us
    dot_general x5, matrix products, local(): jnp.einsum('htu,uhd->thd', weights.astype(jnp.bfloat16), value_heads, pre...  11 us
    dot_general x5, matrix products, masked_scores(): jnp.einsum('thd,uhd->htu', query_heads, key_heads, preferred_element_type...  7.82 us
    dot_general x5, matrix products, local(): jnp.einsum('htu,thd->uhd', probs_low, grad_heads, preferred_element_type=...  5.34 us
  transfers between devices with their start and end apart: 26, of which 8 were waited for; matrix products, arithmetic and copies ran while one was open for 18% of the time, Pallas kernels for 0%

profile of v1, /device:TPU:0, one launch (start us, length us, event | category | flops | bytes accessed | tf_op | source)
XLA Modules:
  0.0 246.4 jit_solution(10164629875464693465)
XLA Ops:
  8.0 3.0 %collective-permute-start.4 = (bf16[128]{0:T(256)(128)(2,1)S(1)}, bf16[128]{0:T(256)(128)(2,1)S(1)}, u32[]{:S(2)}, u32[]{:S(2)}) collective-permute-start(bf16[128]{0:T(256)(128)(2,1)S(1)} %get-tuple-element.40), channel_id=1, source_target_pairs={{0,4},{2,6},{4,0},{6,2},{8,12},{10,14},{12,8},{14,10},{16,20},{18,... | collective-permute-start | bytes 776 | tf_op jit(solution)/shard_map/ppermute | solution.py:16
  10.9 1.6 collective-permute-start.8
  12.5 2.6 %collective-permute-start.12 = (bf16[128]{0:T(256)(128)(2,1)S(1)}, bf16[128]{0:T(256)(128)(2,1)S(1)}, u32[]{:S(2)}, u32[]{:S(2)}) collective-permute-start(bf16[128]{0:T(256)(128)(2,1)S(1)} %get-tuple-element.40), channel_id=1, source_target_pairs={{0,16},{2,18},{4,20},{6,22},{8,24},{10,26},{12,28},{14,30},{16,0},... | collective-permute-start | bytes 776 | tf_op jit(solution)/shard_map/ppermute | solution.py:16
  15.8 1.7 collective-permute-start.14
  17.5 1.1 copy.81
  20.9 1.1 copy.66
  22.0 1.1 copy.67
  23.2 1.8 collective-permute-start.10
  25.8 1.0 collective-permute-done.10
  26.7 1.8 collective-permute-start.6
  30.2 0.8 collective-permute-start.2
  31.8 2.6 %collective-permute-start.13 = (bf16[128,1024]{1,0:T(8,128)(2,1)}, bf16[128,1024]{1,0:T(8,128)(2,1)S(1)}, u32[]{:S(2)}, u32[]{:S(2)}) collective-permute-start(bf16[128,1024]{1,0:T(8,128)(2,1)} %bitcast.15), channel_id=1, source_target_pairs={{0,16},{2,18},{4,20},{6,22},{8,24},{10,26},{12,28},{14,30},{16,0},... | collective-permute-start | bytes 786440 | tf_op jit(solution)/shard_map/ppermute | solution.py:16
  36.4 1.2 collective-permute-start.5
  38.0 2.6 %broadcast_compare_fusion = (pred[128,128]{0,1:T(8,128)(4,1)S(1)}, pred[128,128]{0,1:T(8,128)(4,1)S(1)}, pred[128,128]{0,1:T(8,128)(4,1)S(1)}, pred[128,128]{0,1:T(8,128)(4,1)S(1)}, pred[128,128]{0,1:T(8,128)(4,1)S(1)}) fusion(f32[128]{0:T(128)S(1)} %get-tuple-element.41, pred[]{:T(512)} %bitcast.25, f32[128]{0:T(128)S(1)} %convert_element_type.245, ...), kind=kLoop, calls=%fused_computation.151 | loop fusion | flops 147456 | bytes 84484 | tf_op jit(solution)/shard_map/eq | solution.py:43
  41.1 6.8 %collective-permute-done.13 = bf16[128,1024]{1,0:T(8,128)(2,1)S(1)} collective-permute-done((bf16[128,1024]{1,0:T(8,128)(2,1)}, bf16[128,1024]{1,0:T(8,128)(2,1)S(1)}, u32[]{:S(2)}, u32[]{:S(2)}) %collective-permute-start.13) | collective-permute-done | bytes 262176 | tf_op jit(solution)/shard_map/ppermute | solution.py:16
  47.8 0.8 copy.78
  48.7 1.3 fusion.150
  50.2 1.2 collective-permute-start.7
  51.4 1.8 copy.75
  53.2 2.3 fusion.151
  55.5 1.8 copy.72
  57.3 2.3 fusion.152
  59.6 1.8 copy.69
  61.4 1.5 fusion.153
  64.9 1.1 fusion.16
  66.0 1.8 copy.79
  67.8 2.0 convolution_bitcast_fusion
  69.9 1.8 copy.76
  71.7 2.4 convolution_bitcast_fusion.1
  74.1 1.8 copy.73
  75.8 2.4 convolution_bitcast_fusion.2
  78.3 1.8 copy.70
  80.8 3.1 %multiply_reduce_fusion = (f32[128,16]{0,1:T(8,128)S(1)}, bf16[128,16,64]{0,2,1:T(8,128)(2,1)}) fusion(bf16[128,16,64]{0,2,1:T(8,128)(2,1)S(1)} %bitcast.299, f32[128,16]{0,1:T(8,128)S(1)} %copy-done.24, f32[128,16,64]{0,2,1:T(8,128)} %convolution_bitcast_fusion, f32[128,16]{0,1:T(8,128)S(1)} %copy-done.27, f32[128,16,64]{0,2,1:T(8,128)} %convolution_bitcast_fusion.1, ...), kind=kOutput, calls=%fused_computation.103 | convolution fusion | flops 36042752 | bytes 3997696 | tf_op jit(solution)/shard_map/htu,uhd->thd/dot_general | solution.py:112
  87.0 1.3 fusion.156
  88.3 1.3 fusion.157
  89.6 1.1 fusion.93
  90.7 1.2 fusion.32
  91.9 1.1 fusion.96
  92.9 1.2 fusion.31
  94.1 1.1 fusion.103
  95.6 1.2 convolution_convert_fusion
  96.8 1.2 convolution_convert_fusion.1
  98.0 1.2 convolution_convert_fusion.2
  99.8 1.9 copy.102
  101.6 1.2 fusion.29
  103.9 1.2 fusion.30
  105.1 1.0 fusion.33
  106.1 1.9 copy.103
  108.0 2.9 %collective-permute-start.19 = (bf16[128,1024]{0,1:T(8,128)(2,1)}, bf16[128,1024]{0,1:T(8,128)(2,1)}, u32[]{:S(2)}, u32[]{:S(2)}) collective-permute-start(bf16[128,1024]{0,1:T(8,128)(2,1)} %bitcast.353), channel_id=1, source_target_pairs={{0,16},{2,18},{4,20},{6,22},{8,24},{10,26},{12,28},{14,30},{16,0},... | collective-permute-start | bytes 786440 | tf_op jit(solution)/shard_map/ppermute | solution.py:16
  110.9 0.8 collective-permute-start.17
  111.7 2.0 collective-permute-start.23
  113.8 1.5 multiply_add_fusion
  115.4 1.2 convolution_convert_fusion.3
  116.6 27.3 %all-reduce.3.cloned.1.call-done = f32[16,64,64]{2,1,0:T(8,128)} async-done(((f32[16,64,64]{2,1,0:T(8,128)}), f32[16,64,64]{2,1,0:T(8,128)}) %all-reduce.3.cloned.1.call-update) | async-done | bytes 262160 | tf_op jit(solution)/shard_map/psum | solution.py:172
  143.9 0.9 copy-done.21
  144.8 1.5 collective-permute-start.22
  146.3 1.5 collective-permute-start.21
  147.8 1.4 fusion.61
  149.2 3.7 %collective-permute-done.22 = bf16[128,1024]{0,1:T(8,128)(2,1)S(1)} collective-permute-done((bf16[128,1024]{0,1:T(8,128)(2,1)S(1)}, bf16[128,1024]{0,1:T(8,128)(2,1)S(1)}, u32[]{:S(2)}, u32[]{:S(2)}) %collective-permute-start.22) | collective-permute-done | bytes 262176 | tf_op jit(solution)/shard_map/ppermute | solution.py:16
  152.9 1.2 collective-permute-done.21
  154.3 0.8 copy.104
  155.1 0.8 copy.105
  156.0 81.8 %all-reduce.5.cloned.1.call-done = f32[16,64,64]{2,1,0:T(8,128)} async-done(((f32[16,64,64]{2,1,0:T(8,128)}), f32[16,64,64]{2,1,0:T(8,128)}) %all-reduce.5.cloned.1.call-update) | async-done | bytes 262160 | tf_op jit(solution)/shard_map/psum | solution.py:172
  237.7 1.9 copy.135
  (133 shorter events, 15.1 us)
Async XLA Ops:
  7.2 12.0 %copy-start = (bf16[16,64,64]{2,1,0:T(8,128)(2,1)S(1)}, bf16[16,64,64]{2,1,0:T(8,128)(2,1)}, u32[]{:S(2)}) copy-start(bf16[16,64,64]{2,1,0:T(8,128)(2,1)} %param.15) | copy-start | bytes 393220
  7.2 136.7 %all-reduce.3.cloned.1.call-start = ((), (), s32[]{:S(2)}) async-start(), calls=%async_computation | async-start | bytes 1048576 | tf_op jit(solution)/shard_map/psum | solution.py:172
  8.0 27.9 %collective-permute-start.4 = (bf16[128]{0:T(256)(128)(2,1)S(1)}, bf16[128]{0:T(256)(128)(2,1)S(1)}, u32[]{:S(2)}, u32[]{:S(2)}) collective-permute-start(bf16[128]{0:T(256)(128)(2,1)S(1)} %get-tuple-element.40), channel_id=1, source_target_pairs={{0,4},{2,6},{4,0},{6,2},{8,12},{10,14},{12,8},{14,10},{16,20},{18,... | collective-permute-start | bytes 776 | tf_op jit(solution)/shard_map/ppermute | solution.py:16
  10.9 25.5 %collective-permute-start.8 = (bf16[128]{0:T(256)(128)(2,1)S(1)}, bf16[128]{0:T(256)(128)(2,1)S(1)}, u32[]{:S(2)}, u32[]{:S(2)}) collective-permute-start(bf16[128]{0:T(256)(128)(2,1)S(1)} %get-tuple-element.40), channel_id=1, source_target_pairs={{0,8},{2,10},{4,12},{6,14},{8,0},{10,2},{12,4},{14,6},{16,24},{18,... | collective-permute-start | bytes 776 | tf_op jit(solution)/shard_map/ppermute | solution.py:16
  12.5 25.1 %collective-permute-start.12 = (bf16[128]{0:T(256)(128)(2,1)S(1)}, bf16[128]{0:T(256)(128)(2,1)S(1)}, u32[]{:S(2)}, u32[]{:S(2)}) collective-permute-start(bf16[128]{0:T(256)(128)(2,1)S(1)} %get-tuple-element.40), channel_id=1, source_target_pairs={{0,16},{2,18},{4,20},{6,22},{8,24},{10,26},{12,28},{14,30},{16,0},... | collective-permute-start | bytes 776 | tf_op jit(solution)/shard_map/ppermute | solution.py:16
  15.1 22.5 %collective-permute-start = (bf16[128]{0:T(256)(128)(2,1)S(1)}, bf16[128]{0:T(256)(128)(2,1)S(1)}, u32[]{:S(2)}, u32[]{:S(2)}) collective-permute-start(bf16[128]{0:T(256)(128)(2,1)S(1)} %get-tuple-element.40), channel_id=1, source_target_pairs={{0,2},{2,0},{4,6},{6,4},{8,10},{10,8},{12,14},{14,12},{16,18},{18,... | collective-permute-start | bytes 776 | tf_op jit(solution)/shard_map/ppermute | solution.py:16
  15.8 7.4 %collective-permute-start.14 = (bf16[1]{0:T(256)(128)(2,1)}, bf16[1]{0:T(256)(128)(2,1)}, u32[]{:S(2)}, u32[]{:S(2)}) collective-permute-start(bf16[1]{0:T(256)(128)(2,1)} %bitcast.17), channel_id=1, source_target_pairs={{0,16},{2,18},{4,20},{6,22},{8,24},{10,26},{12,28},{14,30},{16,0},... | collective-permute-start | bytes 14 | tf_op jit(solution)/shard_map/ppermute | solution.py:16
  18.6 1.0 copy-start.22
  19.5 0.7 copy-start.33
  23.2 3.6 %collective-permute-start.10 = (bf16[1]{0:T(256)(128)(2,1)}, bf16[1]{0:T(256)(128)(2,1)}, u32[]{:S(2)}, u32[]{:S(2)}) collective-permute-start(bf16[1]{0:T(256)(128)(2,1)} %bitcast.17), channel_id=1, source_target_pairs={{0,8},{2,10},{4,12},{6,14},{8,0},{10,2},{12,4},{14,6},{16,24},{18,... | collective-permute-start | bytes 14 | tf_op jit(solution)/shard_map/ppermute | solution.py:16
  26.7 3.5 %collective-permute-start.6 = (bf16[1]{0:T(256)(128)(2,1)}, bf16[1]{0:T(256)(128)(2,1)}, u32[]{:S(2)}, u32[]{:S(2)}) collective-permute-start(bf16[1]{0:T(256)(128)(2,1)} %bitcast.17), channel_id=1, source_target_pairs={{0,4},{2,6},{4,0},{6,2},{8,12},{10,14},{12,8},{14,10},{16,20},{18,... | collective-permute-start | bytes 14 | tf_op jit(solution)/shard_map/ppermute | solution.py:16
  30.2 1.6 collective-permute-start.2
  31.8 16.0 %collective-permute-start.13 = (bf16[128,1024]{1,0:T(8,128)(2,1)}, bf16[128,1024]{1,0:T(8,128)(2,1)S(1)}, u32[]{:S(2)}, u32[]{:S(2)}) collective-permute-start(bf16[128,1024]{1,0:T(8,128)(2,1)} %bitcast.15), channel_id=1, source_target_pairs={{0,16},{2,18},{4,20},{6,22},{8,24},{10,26},{12,28},{14,30},{16,0},... | collective-permute-start | bytes 786440 | tf_op jit(solution)/shard_map/ppermute | solution.py:16
  35.8 14.4 %collective-permute-start.9 = (bf16[128,1024]{1,0:T(8,128)(2,1)}, bf16[128,1024]{1,0:T(8,128)(2,1)}, u32[]{:S(2)}, u32[]{:S(2)}) collective-permute-start(bf16[128,1024]{1,0:T(8,128)(2,1)} %bitcast.15), channel_id=1, source_target_pairs={{0,8},{2,10},{4,12},{6,14},{8,0},{10,2},{12,4},{14,6},{16,24},{18,... | collective-permute-start | bytes 786440 | tf_op jit(solution)/shard_map/ppermute | solution.py:16
  36.4 19.1 %collective-permute-start.5 = (bf16[128,1024]{1,0:T(8,128)(2,1)}, bf16[128,1024]{1,0:T(8,128)(2,1)}, u32[]{:S(2)}, u32[]{:S(2)}) collective-permute-start(bf16[128,1024]{1,0:T(8,128)(2,1)} %bitcast.15), channel_id=1, source_target_pairs={{0,4},{2,6},{4,0},{6,2},{8,12},{10,14},{12,8},{14,10},{16,20},{18,... | collective-permute-start | bytes 786440 | tf_op jit(solution)/shard_map/ppermute | solution.py:16
  37.6 22.0 %collective-permute-start.1 = (bf16[128,1024]{1,0:T(8,128)(2,1)}, bf16[128,1024]{1,0:T(8,128)(2,1)}, u32[]{:S(2)}, u32[]{:S(2)}) collective-permute-start(bf16[128,1024]{1,0:T(8,128)(2,1)} %bitcast.15), channel_id=1, source_target_pairs={{0,2},{2,0},{4,6},{6,4},{8,10},{10,8},{12,14},{14,12},{16,18},{18,... | collective-permute-start | bytes 786440 | tf_op jit(solution)/shard_map/ppermute | solution.py:16
  37.6 28.4 %collective-permute-start.15 = (bf16[128,1024]{1,0:T(8,128)(2,1)}, bf16[128,1024]{1,0:T(8,128)(2,1)}, u32[]{:S(2)}, u32[]{:S(2)}) collective-permute-start(bf16[128,1024]{1,0:T(8,128)(2,1)} %bitcast.22), channel_id=1, source_target_pairs={{0,16},{2,18},{4,20},{6,22},{8,24},{10,26},{12,28},{14,30},{16,0},... | collective-permute-start | bytes 786440 | tf_op jit(solution)/shard_map/ppermute | solution.py:16
  47.8 22.0 %collective-permute-start.11 = (bf16[128,1024]{1,0:T(8,128)(2,1)}, bf16[128,1024]{1,0:T(8,128)(2,1)}, u32[]{:S(2)}, u32[]{:S(2)}) collective-permute-start(bf16[128,1024]{1,0:T(8,128)(2,1)} %bitcast.22), channel_id=1, source_target_pairs={{0,8},{2,10},{4,12},{6,14},{8,0},{10,2},{12,4},{14,6},{16,24},{18,... | collective-permute-start | bytes 786440 | tf_op jit(solution)/shard_map/ppermute | solution.py:16
  50.2 23.9 %collective-permute-start.7 = (bf16[128,1024]{1,0:T(8,128)(2,1)}, bf16[128,1024]{1,0:T(8,128)(2,1)}, u32[]{:S(2)}, u32[]{:S(2)}) collective-permute-start(bf16[128,1024]{1,0:T(8,128)(2,1)} %bitcast.22), channel_id=1, source_target_pairs={{0,4},{2,6},{4,0},{6,2},{8,12},{10,14},{12,8},{14,10},{16,20},{18,... | collective-permute-start | bytes 786440 | tf_op jit(solution)/shard_map/ppermute | solution.py:16
  55.5 22.8 %collective-permute-start.3 = (bf16[128,1024]{1,0:T(8,128)(2,1)}, bf16[128,1024]{1,0:T(8,128)(2,1)}, u32[]{:S(2)}, u32[]{:S(2)}) collective-permute-start(bf16[128,1024]{1,0:T(8,128)(2,1)} %bitcast.22), channel_id=1, source_target_pairs={{0,2},{2,0},{4,6},{6,4},{8,10},{10,8},{12,14},{14,12},{16,18},{18,... | collective-permute-start | bytes 786440 | tf_op jit(solution)/shard_map/ppermute | solution.py:16
  61.4 1.7 copy-start.1
  61.4 1.7 copy-start.3
  62.9 1.0 copy-start.5
  78.3 1.8 copy-start.25
  78.3 1.8 copy-start.26
  78.3 1.8 copy-start.27
  80.1 0.7 copy-start.24
  80.8 3.1 %copy-start.18 = (bf16[128,1024]{0,1:T(8,128)(2,1)S(1)}, bf16[128,1024]{0,1:T(8,128)(2,1)}, u32[]{:S(2)}) copy-start(bf16[128,1024]{0,1:T(8,128)(2,1)} %copy.79) | copy-start | bytes 786436
  83.9 1.2 copy-start.2
  83.9 1.3 copy-start.19
  85.7 1.2 copy-start.6
  85.7 1.3 copy-start.23
  87.0 1.3 copy-start.4
  87.0 1.3 copy-start.17
  88.3 1.3 copy-start.14
  90.7 1.2 copy-start.16
  99.8 1.9 copy-start.9
  101.6 1.2 copy-start.12
  101.6 1.2 copy-start.15
  102.8 1.0 copy-start.8
  102.8 2.2 copy-start.13
  103.9 1.2 copy-start.10
  103.9 1.2 copy-start.11
  105.1 8.6 %copy-start.28 = (f32[64]{0:T(128)S(1)}, f32[64]{0:T(128)}, u32[]{:S(2)}) copy-start(f32[64]{0:T(128)} %fusion.128) | copy-start | bytes 772
  105.1 8.7 %copy-start.29 = (f32[64]{0:T(128)S(1)}, f32[64]{0:T(128)}, u32[]{:S(2)}) copy-start(f32[64]{0:T(128)} %get-tuple-element.68) | copy-start | bytes 772
  105.1 8.7 %copy-start.30 = (f32[64]{0:T(128)S(1)}, f32[64]{0:T(128)}, u32[]{:S(2)}) copy-start(f32[64]{0:T(128)} %get-tuple-element.69) | copy-start | bytes 772
  105.1 8.7 %copy-start.31 = (f32[64]{0:T(128)S(1)}, f32[64]{0:T(128)}, u32[]{:S(2)}) copy-start(f32[64]{0:T(128)} %get-tuple-element.70) | copy-start | bytes 772
  105.1 8.7 %copy-start.32 = (f32[64]{0:T(128)S(1)}, f32[64]{0:T(128)}, u32[]{:S(2)}) copy-start(f32[64]{0:T(128)} %get-tuple-element.71) | copy-start | bytes 772
  106.1 9.3 %copy-start.7 = (f32[16,128,128]{1,2,0:T(8,128)S(1)}, f32[16,128,128]{1,2,0:T(8,128)}, u32[]{:S(2)}) copy-start(f32[16,128,128]{1,2,0:T(8,128)} %copy-done.5) | copy-start | bytes 3145732
  108.0 35.9 %collective-permute-start.19 = (bf16[128,1024]{0,1:T(8,128)(2,1)}, bf16[128,1024]{0,1:T(8,128)(2,1)}, u32[]{:S(2)}, u32[]{:S(2)}) collective-permute-start(bf16[128,1024]{0,1:T(8,128)(2,1)} %bitcast.353), channel_id=1, source_target_pairs={{0,16},{2,18},{4,20},{6,22},{8,24},{10,26},{12,28},{14,30},{16,0},... | collective-permute-start | bytes 786440 | tf_op jit(solution)/shard_map/ppermute | solution.py:16
  110.9 35.4 %collective-permute-start.18 = (bf16[128,1024]{0,1:T(8,128)(2,1)}, bf16[128,1024]{0,1:T(8,128)(2,1)}, u32[]{:S(2)}, u32[]{:S(2)}) collective-permute-start(bf16[128,1024]{0,1:T(8,128)(2,1)} %bitcast.352), channel_id=1, source_target_pairs={{0,8},{2,10},{4,12},{6,14},{8,0},{10,2},{12,4},{14,6},{16,24},{18,... | collective-permute-start | bytes 786440 | tf_op jit(solution)/shard_map/ppermute | solution.py:16
  110.9 36.9 %collective-permute-start.17 = (bf16[128,1024]{0,1:T(8,128)(2,1)}, bf16[128,1024]{0,1:T(8,128)(2,1)}, u32[]{:S(2)}, u32[]{:S(2)}) collective-permute-start(bf16[128,1024]{0,1:T(8,128)(2,1)} %bitcast.355), channel_id=1, source_target_pairs={{0,4},{2,6},{4,0},{6,2},{8,12},{10,14},{12,8},{14,10},{16,20},{18,... | collective-permute-start | bytes 786440 | tf_op jit(solution)/shard_map/ppermute | solution.py:16
  111.7 36.1 %collective-permute-start.16 = (bf16[128,1024]{0,1:T(8,128)(2,1)}, bf16[128,1024]{0,1:T(8,128)(2,1)}, u32[]{:S(2)}, u32[]{:S(2)}) collective-permute-start(bf16[128,1024]{0,1:T(8,128)(2,1)} %bitcast.354), channel_id=1, source_target_pairs={{0,2},{2,0},{4,6},{6,4},{8,10},{10,8},{12,14},{14,12},{16,18},{18,... | collective-permute-start | bytes 786440 | tf_op jit(solution)/shard_map/ppermute | solution.py:16
  111.7 37.5 %collective-permute-start.23 = (bf16[128,1024]{0,1:T(8,128)(2,1)}, bf16[128,1024]{0,1:T(8,128)(2,1)S(1)}, u32[]{:S(2)}, u32[]{:S(2)}) collective-permute-start(bf16[128,1024]{0,1:T(8,128)(2,1)} %bitcast.343), channel_id=1, source_target_pairs={{0,16},{2,18},{4,20},{6,22},{8,24},{10,26},{12,28},{14,30},{16,0},... | collective-permute-start | bytes 786440 | tf_op jit(solution)/shard_map/ppermute | solution.py:16
  115.4 122.4 %all-reduce.5.cloned.1.call-start = ((), (), s32[]{:S(2)}) async-start(), calls=%async_computation.1 | async-start | bytes 1048576 | tf_op jit(solution)/shard_map/psum | solution.py:172
  143.9 0.9 copy-start.21
  143.9 2.4 copy-start.20
  144.8 8.0 %collective-permute-start.22 = (bf16[128,1024]{0,1:T(8,128)(2,1)S(1)}, bf16[128,1024]{0,1:T(8,128)(2,1)S(1)}, u32[]{:S(2)}, u32[]{:S(2)}) collective-permute-start(bf16[128,1024]{0,1:T(8,128)(2,1)S(1)} %bitcast.342), channel_id=1, source_target_pairs={{0,8},{2,10},{4,12},{6,14},{8,0},{10,2},{12,4},{14,6},{16,24},{18,... | collective-permute-start | bytes 786440 | tf_op jit(solution)/shard_map/ppermute | solution.py:16
  146.3 7.8 %collective-permute-start.21 = (bf16[128,1024]{0,1:T(8,128)(2,1)S(1)}, bf16[128,1024]{0,1:T(8,128)(2,1)S(1)}, u32[]{:S(2)}, u32[]{:S(2)}) collective-permute-start(bf16[128,1024]{0,1:T(8,128)(2,1)S(1)} %bitcast.341), channel_id=1, source_target_pairs={{0,4},{2,6},{4,0},{6,2},{8,12},{10,14},{12,8},{14,10},{16,20},{18,... | collective-permute-start | bytes 786440 | tf_op jit(solution)/shard_map/ppermute | solution.py:16
  147.8 6.3 %collective-permute-start.20 = (bf16[128,1024]{0,1:T(8,128)(2,1)}, bf16[128,1024]{0,1:T(8,128)(2,1)S(1)}, u32[]{:S(2)}, u32[]{:S(2)}) collective-permute-start(bf16[128,1024]{0,1:T(8,128)(2,1)} %bitcast.345), channel_id=1, source_target_pairs={{0,2},{2,0},{4,6},{6,4},{8,10},{10,8},{12,14},{14,12},{16,18},{18,... | collective-permute-start | bytes 786440 | tf_op jit(solution)/shard_map/ppermute | solution.py:16
Sparse Core Ops, SparseCore 0:
  115.5 28.3 all-reduce.2
  147.6 90.0 all-reduce.4
